TPU v7x, 32 devices: a whole 2x2x4 slice. The times are simulated.
32 devices in a mesh: chan: 8 (over z, x), bl: 4 (over y, core).
Axes of the slice: x: 2, y: 2, z: 4, core: 2. Of those that a mesh axis runs over, the one named last changes fastest.
Arguments:
- visibilities: bfloat16 [1024, 1536, 2, 128], P('bl', 'chan'), may hold values from -6 to 6
- kernels: bfloat16 [64, 128, 256], replicated, may hold values from -0.1875 to 0.1875
- block_ids: int32 [4, 64, 8], P('bl'), may hold values from 0 to 255
- kernel_ids: int32 [4, 64, 8], P('bl'), may hold values from 0 to 63
- tile_counts: int32 [4, 64], P('bl'), may hold values from 1 to 8, as said below
- wedge_mask: int32 [64, 1536], P(('chan', 'bl')), may hold values 0 or 1
Outputs:
- delay_tiles: float32 [64, 2, 256, 1536], P(('chan', 'bl'))
Inputs may be any that keep to these rules, and one draw needn't show every extreme that they name: `tile_counts`: slots at or past a tile's count are ignored; in every group some tile uses all 8 slots.
All inputs are finite; a program needn't handle non-finite values. No bound on the sum of `wedge_mask` on one device may be relied on, other than what follows from the above.
Results may differ from a plain program's by a relative error of at most 0.0095.
Values may be sent and summed in bfloat16 or wider, within the bound.
No kernel may reach another device: no remote copies, remote signals or barrier semaphores. Data moves between devices by JAX's collectives and lax.ppermute only.
A program may use at most 192 MiB of HBM per device.

v0:
```python
import math
import jax
import jax.numpy as jnp
from jax import lax
from jax.sharding import PartitionSpec as P


def delay_tables(nchan):
    chans = jnp.arange(nchan, dtype=jnp.int32)
    phase = chans[:, None] * chans[None, :] % nchan
    angle = phase.astype(jnp.float32) * (2.0 * math.pi / nchan)
    return (jnp.cos(angle).astype(jnp.bfloat16), jnp.sin(angle).astype(jnp.bfloat16))


def grid_tiles(vis_blocks, kernels, list_ids, list_kernels, list_counts):
    tiles, depth = list_ids.shape
    group_size = 16
    row_count = vis_blocks.shape[1]
    cells = kernels.shape[2]
    slots = jnp.arange(depth, dtype=jnp.int32)

    def one_group(inputs):
        group_ids, group_kernels, group_counts = inputs
        keep = (slots[None, :] < group_counts[:, None]).astype(jnp.bfloat16)
        total = jnp.zeros((group_size, row_count, cells), jnp.float32)
        for slot in range(depth):
            chosen = jnp.take(vis_blocks, group_ids[:, slot], axis=0)
            weights = (
                jnp.take(kernels, group_kernels[:, slot], axis=0) * keep[:, slot][:, None, None]
            )
            total = total + jnp.einsum(
                "trs,tsx->trx", chosen, weights, preferred_element_type=jnp.float32
            )
        return total.astype(jnp.bfloat16)

    shaped = (
        list_ids.reshape(tiles // group_size, group_size, depth),
        list_kernels.reshape(tiles // group_size, group_size, depth),
        list_counts.reshape(tiles // group_size, group_size),
    )
    return lax.map(one_group, shaped)


def local(visibilities, kernels, block_ids, kernel_ids, tile_counts, wedge_mask):
    n_chan = lax.axis_size("chan")
    n_group = lax.axis_size("bl")
    nblocks = visibilities.shape[0]
    ch_dev = visibilities.shape[1]
    block_len = kernels.shape[1]
    cells = kernels.shape[2]
    vis_blocks = visibilities.reshape(nblocks, ch_dev * 2, block_len)
    list_ids = block_ids[0]
    list_kernels = kernel_ids[0]
    list_counts = tile_counts[0]
    tiles = list_ids.shape[0]
    owned = wedge_mask.shape[0]
    order = jnp.arange(tiles, dtype=jnp.int32)
    group_of = order // (n_chan * owned)
    column = order // owned % n_chan
    inner = order % owned
    source = (column * n_group + group_of) * owned + inner
    list_ids = jnp.take(list_ids, source, axis=0)
    list_kernels = jnp.take(list_kernels, source, axis=0)
    list_counts = jnp.take(list_counts, source, axis=0)
    partial_value = grid_tiles(vis_blocks, kernels, list_ids, list_kernels, list_counts)
    partial_value = partial_value.reshape(tiles, ch_dev, 2, cells)
    summed = lax.psum_scatter(partial_value, "bl", scatter_dimension=0, tiled=True).astype(
        jnp.float32
    )
    gridded = lax.all_to_all(
        summed.astype(jnp.bfloat16), "chan", split_axis=0, concat_axis=1, tiled=True
    )
    nchan = gridded.shape[1]
    cosine, sine = delay_tables(nchan)
    real_part = gridded[:, :, 0]
    imag_part = gridded[:, :, 1]
    out_real = jnp.einsum(
        "tcx,cd->txd", real_part, cosine, preferred_element_type=jnp.float32
    ) + jnp.einsum("tcx,cd->txd", imag_part, sine, preferred_element_type=jnp.float32)
    out_imag = jnp.einsum(
        "tcx,cd->txd", imag_part, cosine, preferred_element_type=jnp.float32
    ) - jnp.einsum("tcx,cd->txd", real_part, sine, preferred_element_type=jnp.float32)
    scale = 1.0 / math.sqrt(nchan)
    keep_bins = wedge_mask.astype(jnp.float32)
    return jnp.stack([out_real, out_imag], axis=1) * scale * keep_bins[:, None, None, :]


def solution(mesh):
    return jax.shard_map(
        local,
        mesh=mesh,
        in_specs=(
            P("bl", "chan", None, None),
            P(),
            P("bl", None, None),
            P("bl", None, None),
            P("bl", None),
            P(("chan", "bl"), None),
        ),
        out_specs=P(("chan", "bl"), None, None, None),
        check_vma=False,
    )
```

profile of v0, /device:TPU:0, one launch (start us, length us, event | category | flops | bytes accessed | tf_op | source)
XLA Modules:
  0.0 936.1 jit_solution(17992654445042598032)
XLA Ops:
  10.5 572.3 %while.11 = (s32[]{:T(128)}, bf16[4,16,384,256]{3,1,0,2:T(8,128)(2,1)}, s32[4,16,8]{1,2,0:T(8,128)S(1)}, bf16[256,384,128]{2,1,0:T(8,128)(2,1)}, s32[4,16,8]{1,2...) while((s32[]{:T(128)}, ...), condition=%wide.region_1.5_spmd.clone, body=%wide.region_0.4_spmd.clone.sunk | while | flops 3248506624 | bytes 160506144 | solution.py:41
  10.6 9.0 gather_fusion.2
  26.1 9.0 gather_fusion.4
  41.6 9.0 gather_fusion.6
  53.4 3.8 fusion.173
  57.2 9.0 gather_fusion.8
  69.0 3.8 fusion.174
  72.8 9.0 gather_fusion.10
  84.7 3.7 fusion.175
  88.4 9.0 gather_fusion.12
  103.8 9.0 gather_fusion
  115.7 3.8 fusion.170
  119.4 10.0 %gather_fusion.14 = bf16[16,384,128]{2,1,0:T(8,128)(2,1)} fusion(bf16[256,384,128]{2,1,0:T(8,128)(2,1)} %get-tuple-element.327, s32[1024]{0:T(1024)S(1)} %pad_clamp_fusion.48), kind=kCustom, calls=%fused_computation.10.clone.clone.1 | custom fusion | bytes 3145792 | tf_op jit(solution)/shard_map/while/body/eval_jaxpr/jit(_take)/gather | solution.py:27
  129.5 3.8 gather_fusion.15
  133.3 16.6 %fusion.177 = bf16[1,16,384,256]{3,2,1,0:T(8,128)(2,1)S(1)} fusion(f32[16,384,256]{2,1,0:T(8,128)} %fusion.170, f32[16,384,256]{2,1,0:T(8,128)} %fusion.171, f32[16,384,256]{2,1,0:T(8,128)} %fusion.172, f32[16,384,256]{2,1,0:T(8,128)} %fusion.173, f32[16,384,256]{2,1,0:T(8,128)} %fusion.174, f32[16,384,256]{2,1,0:T(8,128)} %fusion.175, ...), kind=kOutput, calls=%fused_computation.21.clone.1 | convolution fusion | flops 417071104 | bytes 49807424 | tf_op jit(solution)/shard_map/while/body/eval_jaxpr/trs,tsx->trx/dot_general | solution.py:31
  153.5 9.0 gather_fusion.2
  169.1 9.0 gather_fusion.4
  184.6 9.0 gather_fusion.6
  196.4 3.7 fusion.173
  200.2 9.0 gather_fusion.8
  212.0 3.8 fusion.174
  215.8 9.0 gather_fusion.10
  231.3 9.0 gather_fusion.12
  246.8 9.0 gather_fusion
  258.6 3.8 fusion.170
  262.4 10.0 %gather_fusion.14 = bf16[16,384,128]{2,1,0:T(8,128)(2,1)} fusion(bf16[256,384,128]{2,1,0:T(8,128)(2,1)} %get-tuple-element.327, s32[1024]{0:T(1024)S(1)} %pad_clamp_fusion.48), kind=kCustom, calls=%fused_computation.10.clone.clone.1 | custom fusion | bytes 3145792 | tf_op jit(solution)/shard_map/while/body/eval_jaxpr/jit(_take)/gather | solution.py:27
  272.5 3.8 gather_fusion.15
  276.2 16.6 %fusion.177 = bf16[1,16,384,256]{3,2,1,0:T(8,128)(2,1)S(1)} fusion(f32[16,384,256]{2,1,0:T(8,128)} %fusion.170, f32[16,384,256]{2,1,0:T(8,128)} %fusion.171, f32[16,384,256]{2,1,0:T(8,128)} %fusion.172, f32[16,384,256]{2,1,0:T(8,128)} %fusion.173, f32[16,384,256]{2,1,0:T(8,128)} %fusion.174, f32[16,384,256]{2,1,0:T(8,128)} %fusion.175, ...), kind=kOutput, calls=%fused_computation.21.clone.1 | convolution fusion | flops 417071104 | bytes 49807424 | tf_op jit(solution)/shard_map/while/body/eval_jaxpr/trs,tsx->trx/dot_general | solution.py:31
  296.5 9.0 gather_fusion.2
  312.1 9.0 gather_fusion.4
  327.6 9.0 gather_fusion.6
  339.4 3.7 fusion.173
  343.2 9.0 gather_fusion.8
  355.0 3.8 fusion.174
  358.8 9.0 gather_fusion.10
  370.6 3.7 fusion.175
  374.3 9.0 gather_fusion.12
  389.8 9.0 gather_fusion
  401.6 3.8 fusion.170
  405.4 10.0 %gather_fusion.14 = bf16[16,384,128]{2,1,0:T(8,128)(2,1)} fusion(bf16[256,384,128]{2,1,0:T(8,128)(2,1)} %get-tuple-element.327, s32[1024]{0:T(1024)S(1)} %pad_clamp_fusion.48), kind=kCustom, calls=%fused_computation.10.clone.clone.1 | custom fusion | bytes 3145792 | tf_op jit(solution)/shard_map/while/body/eval_jaxpr/jit(_take)/gather | solution.py:27
  415.5 3.8 gather_fusion.15
  419.2 16.6 %fusion.177 = bf16[1,16,384,256]{3,2,1,0:T(8,128)(2,1)S(1)} fusion(f32[16,384,256]{2,1,0:T(8,128)} %fusion.170, f32[16,384,256]{2,1,0:T(8,128)} %fusion.171, f32[16,384,256]{2,1,0:T(8,128)} %fusion.172, f32[16,384,256]{2,1,0:T(8,128)} %fusion.173, f32[16,384,256]{2,1,0:T(8,128)} %fusion.174, f32[16,384,256]{2,1,0:T(8,128)} %fusion.175, ...), kind=kOutput, calls=%fused_computation.21.clone.1 | convolution fusion | flops 417071104 | bytes 49807424 | tf_op jit(solution)/shard_map/while/body/eval_jaxpr/trs,tsx->trx/dot_general | solution.py:31
  439.5 9.0 gather_fusion.2
  455.1 9.0 gather_fusion.4
  470.6 9.0 gather_fusion.6
  482.4 3.7 fusion.173
  486.2 9.0 gather_fusion.8
  498.0 3.8 fusion.174
  501.8 9.0 gather_fusion.10
  513.6 3.7 fusion.175
  517.3 9.0 gather_fusion.12
  532.8 9.0 gather_fusion
  544.6 3.8 fusion.170
  548.4 10.0 %gather_fusion.14 = bf16[16,384,128]{2,1,0:T(8,128)(2,1)} fusion(bf16[256,384,128]{2,1,0:T(8,128)(2,1)} %get-tuple-element.327, s32[1024]{0:T(1024)S(1)} %pad_clamp_fusion.48), kind=kCustom, calls=%fused_computation.10.clone.clone.1 | custom fusion | bytes 3145792 | tf_op jit(solution)/shard_map/while/body/eval_jaxpr/jit(_take)/gather | solution.py:27
  558.5 3.8 gather_fusion.15
  562.2 16.6 %fusion.177 = bf16[1,16,384,256]{3,2,1,0:T(8,128)(2,1)S(1)} fusion(f32[16,384,256]{2,1,0:T(8,128)} %fusion.170, f32[16,384,256]{2,1,0:T(8,128)} %fusion.171, f32[16,384,256]{2,1,0:T(8,128)} %fusion.172, f32[16,384,256]{2,1,0:T(8,128)} %fusion.173, f32[16,384,256]{2,1,0:T(8,128)} %fusion.174, f32[16,384,256]{2,1,0:T(8,128)} %fusion.175, ...), kind=kOutput, calls=%fused_computation.21.clone.1 | convolution fusion | flops 417071104 | bytes 49807424 | tf_op jit(solution)/shard_map/while/body/eval_jaxpr/trs,tsx->trx/dot_general | solution.py:31
  582.8 100.0 %reduce-scatter.2.cloned.1.call-done = bf16[16,192,2,256]{3,0,2,1:T(8,128)(2,1)} async-done(((bf16[64,192,2,256]{3,0,2,1:T(8,128)(2,1)}), bf16[16,192,2,256]{3,0,2,1:T(8,128)(2,1)}) %reduce-scatter.2.cloned.1.call-update) | async-done | bytes 3145744 | tf_op jit(solution)/shard_map/reduce_scatter | solution.py:67
  682.8 6.6 copy.35
  689.4 5.6 all-to-all-start
  695.0 70.5 %all-to-all-done = bf16[16,192,2,256]{3,2,1,0:T(2,128)(2,1)S(1)} async-done(((bf16[16,192,2,256]{3,2,1,0:T(2,128)(2,1)}), bf16[16,192,2,256]{3,2,1,0:T(2,128)(2,1)S(1)}, u32[]{:S(2)}, u32[]{:S(2)}) %all-to-all-start) | async-done | bytes 3145760 | tf_op jit(solution)/shard_map/all_to_all | solution.py:70
  766.9 39.4 %fusion.77 = f32[2,256,1536]{2,1,0:T(8,128)S(1)} fusion(bf16[2,1536,256]{2,1,0:T(8,128)(2,1)S(1)} %slice_bitcast_fusion.27), kind=kOutput, calls=%fused_computation.169 | convolution fusion | flops 2439512064 | bytes 4718592 | tf_op jit(solution)/shard_map/tcx,cd->txd/dot_general | solution.py:79
  806.3 39.6 %fusion.75 = f32[2,256,1536]{2,1,0:T(8,128)S(1)} fusion(bf16[2,1536,256]{2,1,0:T(8,128)(2,1)S(1)} %slice_bitcast_fusion.26), kind=kOutput, calls=%fused_computation.168 | convolution fusion | flops 2439512064 | bytes 4718592 | tf_op jit(solution)/shard_map/tcx,cd->txd/dot_general | solution.py:82
  845.9 39.6 %fusion.92 = f32[2,1,256,1536]{3,2,0,1:T(8,128)S(1)} fusion(f32[2,256,1536]{2,1,0:T(8,128)S(1)} %fusion.77, bf16[2,1536,256]{2,1,0:T(8,128)(2,1)S(1)} %slice_bitcast_fusion.29), kind=kOutput, calls=%fused_computation.175 | convolution fusion | flops 2440298496 | bytes 7864320 | tf_op jit(solution)/shard_map/tcx,cd->txd/dot_general | solution.py:77
  885.5 39.4 %fusion.89 = f32[2,1,256,1536]{3,2,0,1:T(8,128)S(1)} fusion(f32[2,256,1536]{2,1,0:T(8,128)S(1)} %fusion.75, bf16[2,1536,256]{2,1,0:T(8,128)(2,1)S(1)} %slice_bitcast_fusion.28), kind=kOutput, calls=%fused_computation.174 | convolution fusion | flops 2440298496 | bytes 7864320 | tf_op jit(solution)/shard_map/tcx,cd->txd/dot_general | solution.py:80
  (166 shorter events, 149.9 us)
Async XLA Ops:
  6.5 3.0 copy-start
  6.5 676.3 %reduce-scatter.2.cloned.1.call-start = ((), (), s32[]{:S(2)}) async-start(), calls=%async_computation.2 | async-start | bytes 15728640 | tf_op jit(solution)/shard_map/reduce_scatter | solution.py:67
  689.4 5.6 copy-start.2
  689.4 76.2 %all-to-all-start = ((bf16[16,192,2,256]{3,2,1,0:T(2,128)(2,1)}), bf16[16,192,2,256]{3,2,1,0:T(2,128)(2,1)S(1)}, u32[]{:S(2)}, u32[]{:S(2)}) async-start(bf16[16,192,2,256]{3,2,1,0:T(2,128)(2,1)} %copy.35), calls=%async_computation.1 | async-start | bytes 6291456 | tf_op jit(solution)/shard_map/all_to_all | solution.py:70
  925.7 3.2 copy-start.1
Sparse Core Ops, SparseCore 0:
  582.9 99.8 reduce-scatter.1
where the time goes:
time: 949 us; the launch traced here: 936 us
  local copies, waits for them, and re-layouts  415 us (44%)
  matrix products  328 us (35%)
  waiting for transfers between devices  171 us (18%)
  between operations  14 us (1%)
    gather x32, local copies, waits for them, and re-layouts, one_group(): chosen = jnp.take(vis_blocks, group_ids[:, slot], axis=0)  292 us
    dot_general x32, matrix products, one_group(): jnp.einsum('trs,tsx->trx', chosen, weights, preferred_element_type=jnp.fl...  170 us
    reduce_scatter x1, waiting for transfers between devices, local(): lax.psum_scatter(partial_value, 'bl', scatter_dimension=0, tiled=True)  100 us
    gather x32, local copies, waits for them, and re-layouts, one_group(): jnp.take(kernels, group_kernels[:, slot], axis=0)  93.6 us
    all_to_all x1, waiting for transfers between devices, local(): lax.all_to_all(summed.astype(jnp.bfloat16), 'chan', split_axis=0, concat_...  70.5 us
    dot_general x1, matrix products, local(): jnp.einsum('tcx,cd->txd', real_part, cosine, preferred_element_type=jnp.f...  39.6 us
    dot_general x1, matrix products, local(): jnp.einsum('tcx,cd->txd', real_part, sine, preferred_element_type=jnp.flo...  39.6 us
    dot_general x1, matrix products, local(): jnp.einsum('tcx,cd->txd', imag_part, cosine, preferred_element_type=jnp.f...  39.4 us
  transfers between devices with their start and end apart: 2, of which 2 were waited for; matrix products, arithmetic and copies ran while one was open for 0% of the time, Pallas kernels for 0%

commit v1 on v0

--- a/solution.py
+++ b/solution.py
@@ -1,8 +1,34 @@
+import functools
 import math
 import jax
 import jax.numpy as jnp
 from jax import lax
 from jax.sharding import PartitionSpec as P
+
+
+def _play_view(array_in, bus_axis):
+    u_next, out_arr = (lax.axis_size(bus_axis), lax.axis_index(bus_axis))
+    prior = array_in.shape[0] // u_next
+    near = list(array_in.shape)
+    near[0] = prior
+    carry = near[1]
+    near[1] = carry * u_next
+    pp = 0
+    everything = jnp.zeros(near, array_in.dtype)
+    while pp < u_next:
+        state_next = lax.dynamic_slice_in_dim(array_in, (out_arr ^ pp) * prior, prior, axis=0)
+        if pp:
+            state_next = lax.ppermute(
+                state_next, axis_name=bus_axis, perm=[(rr, rr ^ pp) for rr in range(u_next)]
+            )
+        everything = lax.dynamic_update_slice_in_dim(
+            everything, state_next, (out_arr ^ pp) * carry, axis=1
+        )
+        pp += 1
+    return everything
+
+
+knots_attach = functools.partial(_play_view, bus_axis="chan")
 
 
 def delay_tables(nchan):
@@ -67,9 +93,7 @@
     summed = lax.psum_scatter(partial_value, "bl", scatter_dimension=0, tiled=True).astype(
         jnp.float32
     )
-    gridded = lax.all_to_all(
-        summed.astype(jnp.bfloat16), "chan", split_axis=0, concat_axis=1, tiled=True
-    )
+    gridded = knots_attach(summed.astype(jnp.bfloat16))
     nchan = gridded.shape[1]
     cosine, sine = delay_tables(nchan)
     real_part = gridded[:, :, 0]

time: 949 us -> 983 us (1.036)
  the two profiles are of different devices: /device:TPU:0 before, /device:TPU:16 now
where the time goes in v1:
time: 983 us; the launch traced here: 968 us
  local copies, waits for them, and re-layouts  485 us (49%)
  matrix products  320 us (33%)
  waiting for transfers between devices  139 us (14%)
  between operations  14.1 us (1%)
    gather x32, local copies, waits for them, and re-layouts, one_group(): chosen = jnp.take(vis_blocks, group_ids[:, slot], axis=0)  292 us
    dot_general x32, matrix products, one_group(): jnp.einsum('trs,tsx->trx', chosen, weights, preferred_element_type=jnp.fl...  170 us
    reduce_scatter x1, waiting for transfers between devices, local(): lax.psum_scatter(partial_value, 'bl', scatter_dimension=0, tiled=True)  101 us
    gather x32, local copies, waits for them, and re-layouts, one_group(): jnp.take(kernels, group_kernels[:, slot], axis=0)  93.5 us
    dynamic_update_slice x8, local copies, waits for them, and re-layouts, _play_view(): lax.dynamic_update_slice_in_dim(everything, state_next, (out_arr ^ pp) *...  53.7 us
    ppermute x7, waiting for transfers between devices, _play_view(): lax.ppermute(state_next, axis_name=bus_axis, perm=[(rr, rr ^ pp) for rr i...  37.7 us
    dot_general x1, matrix products, local(): jnp.einsum('tcx,cd->txd', imag_part, sine, preferred_element_type=jnp.flo...  37.6 us
    dot_general x1, matrix products, local(): jnp.einsum('tcx,cd->txd', real_part, sine, preferred_element_type=jnp.flo...  37.4 us
  transfers between devices with their start and end apart: 8, of which 6 were waited for; matrix products, arithmetic and copies ran while one was open for 5% of the time, Pallas kernels for 0%

profile of v1, /device:TPU:16, one launch (start us, length us, event | category | flops | bytes accessed | tf_op | source)
XLA Modules:
  0.0 968.3 jit_solution(16106050122400893223)
XLA Ops:
  10.5 572.1 %while.11 = (s32[]{:T(128)}, bf16[4,16,384,256]{3,1,0,2:T(8,128)(2,1)}, s32[4,16,8]{1,2,0:T(8,128)S(1)}, bf16[256,384,128]{2,1,0:T(8,128)(2,1)}, s32[4,16,8]{1,2...) while((s32[]{:T(128)}, ...), condition=%wide.region_1.5_spmd.clone, body=%wide.region_0.4_spmd.clone.sunk | while | flops 3248506624 | bytes 160506144 | solution.py:67
  10.6 9.0 gather_fusion.2
  26.1 9.0 gather_fusion.4
  41.6 9.0 gather_fusion.6
  57.2 9.0 gather_fusion.8
  69.1 3.8 fusion.174
  72.8 9.0 gather_fusion.10
  88.4 9.0 gather_fusion.12
  103.9 9.0 gather_fusion
  115.7 3.8 fusion.170
  119.5 10.0 %gather_fusion.14 = bf16[16,384,128]{2,1,0:T(8,128)(2,1)} fusion(bf16[256,384,128]{2,1,0:T(8,128)(2,1)} %get-tuple-element.328, s32[1024]{0:T(1024)S(1)} %pad_clamp_fusion.48), kind=kCustom, calls=%fused_computation.10.clone.clone.1 | custom fusion | bytes 3145792 | tf_op jit(solution)/shard_map/while/body/eval_jaxpr/jit(_take)/gather | solution.py:53
  129.5 3.8 gather_fusion.15
  133.3 16.6 %fusion.177 = bf16[1,16,384,256]{3,2,1,0:T(8,128)(2,1)S(1)} fusion(f32[16,384,256]{2,1,0:T(8,128)} %fusion.170, f32[16,384,256]{2,1,0:T(8,128)} %fusion.171, f32[16,384,256]{2,1,0:T(8,128)} %fusion.172, f32[16,384,256]{2,1,0:T(8,128)} %fusion.173, f32[16,384,256]{2,1,0:T(8,128)} %fusion.174, f32[16,384,256]{2,1,0:T(8,128)} %fusion.175, ...), kind=kOutput, calls=%fused_computation.21.clone.1 | convolution fusion | flops 417071104 | bytes 49807424 | tf_op jit(solution)/shard_map/while/body/eval_jaxpr/trs,tsx->trx/dot_general | solution.py:57
  153.5 9.0 gather_fusion.2
  169.1 9.0 gather_fusion.4
  184.6 9.0 gather_fusion.6
  196.4 3.8 fusion.173
  200.2 9.0 gather_fusion.8
  212.0 3.8 fusion.174
  215.8 9.0 gather_fusion.10
  231.4 9.0 gather_fusion.12
  246.8 9.0 gather_fusion
  262.4 10.0 %gather_fusion.14 = bf16[16,384,128]{2,1,0:T(8,128)(2,1)} fusion(bf16[256,384,128]{2,1,0:T(8,128)(2,1)} %get-tuple-element.328, s32[1024]{0:T(1024)S(1)} %pad_clamp_fusion.48), kind=kCustom, calls=%fused_computation.10.clone.clone.1 | custom fusion | bytes 3145792 | tf_op jit(solution)/shard_map/while/body/eval_jaxpr/jit(_take)/gather | solution.py:53
  272.5 3.8 gather_fusion.15
  276.2 16.6 %fusion.177 = bf16[1,16,384,256]{3,2,1,0:T(8,128)(2,1)S(1)} fusion(f32[16,384,256]{2,1,0:T(8,128)} %fusion.170, f32[16,384,256]{2,1,0:T(8,128)} %fusion.171, f32[16,384,256]{2,1,0:T(8,128)} %fusion.172, f32[16,384,256]{2,1,0:T(8,128)} %fusion.173, f32[16,384,256]{2,1,0:T(8,128)} %fusion.174, f32[16,384,256]{2,1,0:T(8,128)} %fusion.175, ...), kind=kOutput, calls=%fused_computation.21.clone.1 | convolution fusion | flops 417071104 | bytes 49807424 | tf_op jit(solution)/shard_map/while/body/eval_jaxpr/trs,tsx->trx/dot_general | solution.py:57
  296.5 9.0 gather_fusion.2
  312.1 9.0 gather_fusion.4
  327.6 9.0 gather_fusion.6
  343.2 9.0 gather_fusion.8
  355.0 3.8 fusion.174
  358.8 9.0 gather_fusion.10
  374.3 9.0 gather_fusion.12
  389.8 9.0 gather_fusion
  405.4 10.0 %gather_fusion.14 = bf16[16,384,128]{2,1,0:T(8,128)(2,1)} fusion(bf16[256,384,128]{2,1,0:T(8,128)(2,1)} %get-tuple-element.328, s32[1024]{0:T(1024)S(1)} %pad_clamp_fusion.48), kind=kCustom, calls=%fused_computation.10.clone.clone.1 | custom fusion | bytes 3145792 | tf_op jit(solution)/shard_map/while/body/eval_jaxpr/jit(_take)/gather | solution.py:53
  415.5 3.8 gather_fusion.15
  419.2 16.6 %fusion.177 = bf16[1,16,384,256]{3,2,1,0:T(8,128)(2,1)S(1)} fusion(f32[16,384,256]{2,1,0:T(8,128)} %fusion.170, f32[16,384,256]{2,1,0:T(8,128)} %fusion.171, f32[16,384,256]{2,1,0:T(8,128)} %fusion.172, f32[16,384,256]{2,1,0:T(8,128)} %fusion.173, f32[16,384,256]{2,1,0:T(8,128)} %fusion.174, f32[16,384,256]{2,1,0:T(8,128)} %fusion.175, ...), kind=kOutput, calls=%fused_computation.21.clone.1 | convolution fusion | flops 417071104 | bytes 49807424 | tf_op jit(solution)/shard_map/while/body/eval_jaxpr/trs,tsx->trx/dot_general | solution.py:57
  439.5 9.0 gather_fusion.2
  455.1 9.0 gather_fusion.4
  470.6 9.0 gather_fusion.6
  486.2 9.0 gather_fusion.8
  498.0 3.8 fusion.174
  501.8 9.0 gather_fusion.10
  517.3 9.0 gather_fusion.12
  532.8 9.0 gather_fusion
  548.4 10.0 %gather_fusion.14 = bf16[16,384,128]{2,1,0:T(8,128)(2,1)} fusion(bf16[256,384,128]{2,1,0:T(8,128)(2,1)} %get-tuple-element.328, s32[1024]{0:T(1024)S(1)} %pad_clamp_fusion.48), kind=kCustom, calls=%fused_computation.10.clone.clone.1 | custom fusion | bytes 3145792 | tf_op jit(solution)/shard_map/while/body/eval_jaxpr/jit(_take)/gather | solution.py:53
  558.4 3.8 gather_fusion.15
  562.2 16.6 %fusion.177 = bf16[1,16,384,256]{3,2,1,0:T(8,128)(2,1)S(1)} fusion(f32[16,384,256]{2,1,0:T(8,128)} %fusion.170, f32[16,384,256]{2,1,0:T(8,128)} %fusion.171, f32[16,384,256]{2,1,0:T(8,128)} %fusion.172, f32[16,384,256]{2,1,0:T(8,128)} %fusion.173, f32[16,384,256]{2,1,0:T(8,128)} %fusion.174, f32[16,384,256]{2,1,0:T(8,128)} %fusion.175, ...), kind=kOutput, calls=%fused_computation.21.clone.1 | convolution fusion | flops 417071104 | bytes 49807424 | tf_op jit(solution)/shard_map/while/body/eval_jaxpr/trs,tsx->trx/dot_general | solution.py:57
  582.6 14.1 %copy.24 = bf16[64,192,2,256]{3,1,2,0:T(8,128)(2,1)} copy(bf16[64,192,2,256]{3,0,2,1:T(8,128)(2,1)} %bitcast.155) | data formatting | bytes 25165824 | tf_op jit(solution)/shard_map/reshape | solution.py:92
  596.7 101.0 %reduce-scatter.2.cloned.1.call-done = bf16[16,192,2,256]{3,1,2,0:T(8,128)(2,1)} async-done(((bf16[64,192,2,256]{3,1,2,0:T(8,128)(2,1)}), bf16[16,192,2,256]{3,1,2,0:T(8,128)(2,1)}) %reduce-scatter.2.cloned.1.call-update) | async-done | bytes 3145744 | tf_op jit(solution)/shard_map/reduce_scatter | solution.py:93
  715.4 18.7 %collective-permute-done.1 = bf16[2,192,2,256]{1,3,0,2:T(8,128)(2,1)} collective-permute-done((bf16[2,192,2,256]{1,3,0,2:T(8,128)(2,1)S(1)}, bf16[2,192,2,256]{1,3,0,2:T(8,128)(2,1)}, u32[]{:S(2)}, u32[]{:S(2)}) %collective-permute-start.1) | collective-permute-done | bytes 393248 | tf_op jit(solution)/shard_map/ppermute | solution.py:21
  736.0 6.4 dynamic_update_slice.28
  742.4 7.3 dynamic_update_slice.29
  749.6 6.0 dynamic_update_slice.30
  755.7 6.9 dynamic_update_slice.31
  762.6 6.4 dynamic_update_slice.32
  769.0 6.9 collective-permute-done.4
  775.8 7.2 dynamic_update_slice.33
  783.1 6.9 collective-permute-done.5
  790.0 6.3 dynamic_update_slice.34
  800.0 7.2 dynamic_update_slice.35
  807.7 37.6 %fusion.77 = f32[2,256,1536]{2,1,0:T(8,128)S(1)} fusion(bf16[2,1536,256]{1,2,0:T(8,128)(2,1)S(1)} %slice_bitcast_fusion.27), kind=kOutput, calls=%fused_computation.169 | convolution fusion | flops 2439512064 | bytes 4718592 | tf_op jit(solution)/shard_map/tcx,cd->txd/dot_general | solution.py:103
  845.3 37.4 %fusion.75 = f32[2,256,1536]{2,1,0:T(8,128)S(1)} fusion(bf16[2,1536,256]{1,2,0:T(8,128)(2,1)S(1)} %slice_bitcast_fusion.26), kind=kOutput, calls=%fused_computation.168 | convolution fusion | flops 2439512064 | bytes 4718592 | tf_op jit(solution)/shard_map/tcx,cd->txd/dot_general | solution.py:106
  882.7 37.2 %fusion.92 = f32[2,1,256,1536]{3,2,0,1:T(8,128)S(1)} fusion(f32[2,256,1536]{2,1,0:T(8,128)S(1)} %fusion.77, bf16[2,1536,256]{1,2,0:T(8,128)(2,1)S(1)} %slice_bitcast_fusion.29), kind=kOutput, calls=%fused_computation.175 | convolution fusion | flops 2440298496 | bytes 7864320 | tf_op jit(solution)/shard_map/tcx,cd->txd/dot_general | solution.py:101
  919.9 37.2 %fusion.89 = f32[2,1,256,1536]{3,2,0,1:T(8,128)S(1)} fusion(f32[2,256,1536]{2,1,0:T(8,128)S(1)} %fusion.75, bf16[2,1536,256]{1,2,0:T(8,128)(2,1)S(1)} %slice_bitcast_fusion.28), kind=kOutput, calls=%fused_computation.174 | convolution fusion | flops 2440298496 | bytes 7864320 | tf_op jit(solution)/shard_map/tcx,cd->txd/dot_general | solution.py:104
  (194 shorter events, 205.9 us)
Async XLA Ops:
  6.5 3.0 copy-start
  6.5 691.1 %reduce-scatter.2.cloned.1.call-start = ((), (), s32[]{:S(2)}) async-start(), calls=%async_computation.1 | async-start | bytes 15728640 | tf_op jit(solution)/shard_map/reduce_scatter | solution.py:93
  699.7 35.0 %copy-start.2 = (s32[2,1536]{1,0:T(2,128)S(1)}, s32[2,1536]{1,0:T(2,128)}, u32[]{:S(2)}) copy-start(s32[2,1536]{1,0:T(2,128)} %param.19) | copy-start | bytes 36868
  700.7 14.1 %collective-permute-start = (bf16[2,192,2,256]{1,3,0,2:T(8,128)(2,1)}, bf16[2,192,2,256]{1,3,0,2:T(8,128)(2,1)}, u32[]{:S(2)}, u32[]{:S(2)}) collective-permute-start(bf16[2,192,2,256]{1,3,0,2:T(8,128)(2,1)} %copy.37), channel_id=1, source_target_pairs={{0,4},{4,0},{8,12},{12,8},{16,20},{20,16},{24,28},{28,24},{1,5},{5... | collective-permute-start | bytes 1179656 | tf_op jit(solution)/shard_map/ppermute | solution.py:21
  702.4 31.7 %collective-permute-start.1 = (bf16[2,192,2,256]{1,3,0,2:T(8,128)(2,1)S(1)}, bf16[2,192,2,256]{1,3,0,2:T(8,128)(2,1)}, u32[]{:S(2)}, u32[]{:S(2)}) collective-permute-start(bf16[2,192,2,256]{1,3,0,2:T(8,128)(2,1)S(1)} %copy.38), channel_id=1, source_target_pairs={{0,8},{4,12},{8,0},{12,4},{16,24},{20,28},{24,16},{28,20},{1,9},{5... | collective-permute-start | bytes 1179656 | tf_op jit(solution)/shard_map/ppermute | solution.py:21
  705.0 50.7 %collective-permute-start.2 = (bf16[2,192,2,256]{1,3,0,2:T(8,128)(2,1)}, bf16[2,192,2,256]{1,3,0,2:T(8,128)(2,1)}, u32[]{:S(2)}, u32[]{:S(2)}) collective-permute-start(bf16[2,192,2,256]{1,3,0,2:T(8,128)(2,1)} %copy.39), channel_id=1, source_target_pairs={{0,12},{4,8},{8,4},{12,0},{16,28},{20,24},{24,20},{28,16},{1,13},{... | collective-permute-start | bytes 1179656 | tf_op jit(solution)/shard_map/ppermute | solution.py:21
  706.5 56.0 %collective-permute-start.3 = (bf16[2,192,2,256]{1,3,0,2:T(8,128)(2,1)}, bf16[2,192,2,256]{1,3,0,2:T(8,128)(2,1)}, u32[]{:S(2)}, u32[]{:S(2)}) collective-permute-start(bf16[2,192,2,256]{1,3,0,2:T(8,128)(2,1)} %copy.40), channel_id=1, source_target_pairs={{0,16},{4,20},{8,24},{12,28},{16,0},{20,4},{24,8},{28,12},{1,17},{... | collective-permute-start | bytes 1179656 | tf_op jit(solution)/shard_map/ppermute | solution.py:21
  708.1 67.8 %collective-permute-start.4 = (bf16[2,192,2,256]{1,3,0,2:T(8,128)(2,1)}, bf16[2,192,2,256]{1,3,0,2:T(8,128)(2,1)}, u32[]{:S(2)}, u32[]{:S(2)}) collective-permute-start(bf16[2,192,2,256]{1,3,0,2:T(8,128)(2,1)} %copy.41), channel_id=1, source_target_pairs={{0,20},{4,16},{8,28},{12,24},{16,4},{20,0},{24,12},{28,8},{1,21},{... | collective-permute-start | bytes 1179656 | tf_op jit(solution)/shard_map/ppermute | solution.py:21
  714.9 75.1 %collective-permute-start.5 = (bf16[2,192,2,256]{1,3,0,2:T(8,128)(2,1)}, bf16[2,192,2,256]{1,3,0,2:T(8,128)(2,1)}, u32[]{:S(2)}, u32[]{:S(2)}) collective-permute-start(bf16[2,192,2,256]{1,3,0,2:T(8,128)(2,1)} %copy.42), channel_id=1, source_target_pairs={{0,24},{4,28},{8,16},{12,20},{16,8},{20,12},{24,0},{28,4},{1,25},{... | collective-permute-start | bytes 1179656 | tf_op jit(solution)/shard_map/ppermute | solution.py:21
  734.1 65.9 %collective-permute-start.6 = (bf16[2,192,2,256]{1,3,0,2:T(8,128)(2,1)}, bf16[2,192,2,256]{1,3,0,2:T(8,128)(2,1)}, u32[]{:S(2)}, u32[]{:S(2)}) collective-permute-start(bf16[2,192,2,256]{1,3,0,2:T(8,128)(2,1)} %copy.43), channel_id=1, source_target_pairs={{0,28},{4,24},{8,20},{12,16},{16,12},{20,8},{24,4},{28,0},{1,29},{... | collective-permute-start | bytes 1179656 | tf_op jit(solution)/shard_map/ppermute | solution.py:21
  957.8 3.2 copy-start.1
Sparse Core Ops, SparseCore 0:
  596.8 100.8 reduce-scatter.1
